TPU v7x, 512 devices: a whole 4x4x16 slice. The times are simulated.
512 devices in a mesh: wide: 64 (over z, x), narrow: 8 (over y, core).
Axes of the slice: x: 4, y: 4, z: 16, core: 2. Of those that a mesh axis runs over, the one named last changes fastest.
Arguments:
- sublevel_symbol_entries: bfloat16 [1024, 4, 4096], P('wide', None, 'narrow'), may hold values from -160 to 160
- prior_symbol_memory: bfloat16 [1024, 4096], P('wide', 'narrow'), may hold values from -6 to 6
- entry_scaling_multiplier: float32 [4096], P('narrow'), may hold values from 0.25 to 1.75
- entry_scaling_offset: float32 [4096], P('narrow'), may hold values from -4 to 4
- learned_blending: float32 [6, 4096], P(None, 'narrow'), may hold values from 0 to 1
- blending_lowering_coefficients: bfloat16 [4096, 160], P('narrow'), may hold values from -0.09375 to 0.09375
- blending_raising_coefficients: bfloat16 [5, 32, 4096], P(None, None, 'narrow'), may hold values from -1 to 1
- fading_lowering_coefficients: bfloat16 [4096, 64], P('narrow'), may hold values from -0.09375 to 0.09375
- fading_raising_coefficients: bfloat16 [64, 4096], P(None, 'wide'), may hold values from -0.75 to 0.75
- learned_fading: float32 [4096], P('wide'), may hold values from -6 to 1
- immediate_item_premium: float32 [4096], P('wide'), may hold values from -3 to 3
- acceptor_projection: bfloat16 [4096, 4096], P('narrow', 'wide'), may hold values from -0.09375 to 0.09375
- lookup_projection: bfloat16 [4096, 4096], P('narrow', 'wide'), may hold values from -0.09375 to 0.09375
- payload_projection: bfloat16 [4096, 4096], P('narrow', 'wide'), may hold values from -0.09375 to 0.09375
- gating_projection: bfloat16 [4096, 4096], P('narrow', 'wide'), may hold values from -0.09375 to 0.09375
- emission_projection: bfloat16 [4096, 4096], P(None, 'wide'), may hold values from -0.09375 to 0.09375
- group_scaling_multiplier: float32 [4096], P('wide'), may hold values from 0.25 to 1.75
- group_scaling_offset: float32 [4096], P('wide'), may hold values from -4 to 4
- dialogue_group_memory: float32 [262144, 1024], P('wide', 'narrow'), may hold values from -6 to 6
Outputs:
- mixing_output: bfloat16 [1024, 4, 4096], P('narrow', None, 'wide')
- final_state: float32 [262144, 1024], P('wide', 'narrow')
All inputs are finite; a program needn't handle non-finite values.
Results may differ from a plain program's by a relative error of at most 0.034.
Values may be sent and summed in bfloat16 or wider, within the bound.
A program may use at most 64 MiB of HBM per device.

v0:
```python
import jax
import jax.numpy as jnp
from jax import lax
from jax.sharding import PartitionSpec as P

CHANNEL_SPAN = 64
FEATURE_EXTENT = 4096


def per_device(
    sublevel_symbol_entries,
    prior_symbol_memory,
    entry_scaling_multiplier,
    entry_scaling_offset,
    learned_blending,
    blending_lowering_coefficients,
    blending_raising_coefficients,
    fading_lowering_coefficients,
    fading_raising_coefficients,
    learned_fading,
    immediate_item_premium,
    acceptor_projection,
    lookup_projection,
    payload_projection,
    gating_projection,
    emission_projection,
    group_scaling_multiplier,
    group_scaling_offset,
    dialogue_group_memory,
):
    rank = blending_raising_coefficients.shape[1]
    narrow_rows = dialogue_group_memory.shape[1]
    local_width = emission_projection.shape[1]
    group_partition = local_width // CHANNEL_SPAN
    weights = (acceptor_projection, lookup_projection, payload_projection, gating_projection)
    shift_gathered = lax.all_gather(prior_symbol_memory, "wide", axis=0, tiled=True)

    def channel_set_first(block):
        return block.reshape(narrow_rows, group_partition, CHANNEL_SPAN).transpose(1, 2, 0)

    present_symbol = dialogue_group_memory.reshape(
        group_partition, CHANNEL_SPAN, CHANNEL_SPAN, narrow_rows
    )
    previous_rows = prior_symbol_memory
    previous_all = shift_gathered
    results = []
    for index in range(sublevel_symbol_entries.shape[1]):
        floats = sublevel_symbol_entries[:, index : index + 1].astype(jnp.float32)
        totals, squares = lax.psum((jnp.sum(floats, -1), jnp.sum(floats * floats, -1)), "narrow")
        prepare_center = totals[..., None] / FEATURE_EXTENT
        spread = squares[..., None] / FEATURE_EXTENT - prepare_center * prepare_center
        normed = (
            (floats - prepare_center) * lax.rsqrt(spread + 1e-05) * entry_scaling_multiplier
            + entry_scaling_offset
        ).astype(jnp.bfloat16)
        previous = jnp.concatenate([previous_rows[:, None], normed[:, :-1]], 1)
        prepare_normalized_float = normed.astype(jnp.float32)
        prepare_shifted_input = previous.astype(jnp.float32) - prepare_normalized_float
        blended = (prepare_normalized_float + prepare_shifted_input * learned_blending[0]).astype(
            jnp.bfloat16
        )
        partial_mix = jnp.einsum(
            "smd,dr->smr",
            blended,
            blending_lowering_coefficients,
            preferred_element_type=jnp.float32,
        )
        hidden_activation = jnp.tanh(lax.psum(partial_mix, "narrow")).astype(jnp.bfloat16)
        decay_shift = jnp.einsum(
            "smr,rd->smd",
            hidden_activation[..., :rank],
            blending_raising_coefficients[0],
            preferred_element_type=jnp.float32,
        )
        decay_mix = (
            prepare_normalized_float + prepare_shifted_input * (learned_blending[1] + decay_shift)
        ).astype(jnp.bfloat16)
        partial_decay = jnp.einsum(
            "smd,dr->smr",
            decay_mix,
            fading_lowering_coefficients,
            preferred_element_type=jnp.float32,
        )
        decay_hidden = jnp.tanh(lax.psum(partial_decay, "narrow")).astype(jnp.bfloat16)
        small = jnp.concatenate([hidden_activation[..., rank:], decay_hidden], -1)
        prepare_normed_all = lax.all_gather(normed, "wide", axis=0, tiled=True)
        prepare_small_all = lax.all_gather(small, "wide", axis=0, tiled=True)
        normed, normed_all, small_all = (normed, prepare_normed_all, prepare_small_all)
        project_previous_all = previous_all[:, None]
        normalized_float = normed_all.astype(jnp.float32)
        shifted_input = project_previous_all.astype(jnp.float32) - normalized_float
        term_results = []
        for selector_index in range(4):
            low_rank_update = jnp.einsum(
                "smr,rd->smd",
                small_all[..., selector_index * rank : (selector_index + 1) * rank],
                blending_raising_coefficients[selector_index + 1],
                preferred_element_type=jnp.float32,
            )
            mixed_input = (
                normalized_float
                + shifted_input * (learned_blending[selector_index + 2] + low_rank_update)
            ).astype(jnp.bfloat16)
            term_results.append(
                jnp.einsum(
                    "smd,de->sme",
                    mixed_input,
                    weights[selector_index],
                    preferred_element_type=jnp.float32,
                )
            )
        project_transformed_outcome = lax.psum_scatter(
            jnp.concatenate(term_results, -1).astype(jnp.bfloat16),
            "narrow",
            scatter_dimension=0,
            tiled=True,
        ).astype(jnp.float32)
        rows_start = lax.axis_index("narrow") * narrow_rows
        decay_rows = lax.dynamic_slice_in_dim(
            small_all[..., 4 * rank :], rows_start, narrow_rows, 0
        )
        decay_log = learned_fading + jnp.einsum(
            "smr,rd->smd",
            decay_rows,
            fading_raising_coefficients,
            preferred_element_type=jnp.float32,
        )
        shrink_coefficient = jnp.exp(-jnp.exp(decay_log))
        recurrence_present_symbol = present_symbol
        each_group_reward = immediate_item_premium.reshape(group_partition, CHANNEL_SPAN)
        present_acceptor = channel_set_first(project_transformed_outcome[:, 0, :local_width])
        key_now = channel_set_first(
            project_transformed_outcome[:, 0, local_width : 2 * local_width]
        )
        value_now = channel_set_first(
            project_transformed_outcome[:, 0, 2 * local_width : 3 * local_width]
        )
        gate_now = project_transformed_outcome[:, 0, 3 * local_width :]
        forget_now = channel_set_first(shrink_coefficient[:, 0])
        dyadic_tensor = key_now[:, :, None, :] * value_now[:, None, :, :]
        memory_retrieval = jnp.sum(
            present_acceptor[:, :, None, :]
            * (recurrence_present_symbol + each_group_reward[:, :, None, None] * dyadic_tensor),
            1,
        )
        recurrence_present_symbol = (
            forget_now[:, :, None, :] * recurrence_present_symbol + dyadic_tensor
        )
        center = jnp.mean(memory_retrieval, 1, keepdims=True)
        offset = memory_retrieval - center
        scaled = offset * lax.rsqrt(jnp.mean(offset * offset, 1, keepdims=True) + 0.00064)
        squashed_vector = scaled.transpose(2, 0, 1).reshape(narrow_rows, local_width)
        pieces = [
            (
                (squashed_vector * group_scaling_multiplier + group_scaling_offset)
                * jax.nn.silu(gate_now)
            ).astype(jnp.bfloat16)
        ]
        present_symbol = recurrence_present_symbol
        gated = jnp.stack(pieces, 1)
        results.append(
            jnp.einsum(
                "smc,ce->sme",
                lax.all_gather(gated, "wide", axis=2, tiled=True),
                emission_projection,
                preferred_element_type=jnp.float32,
            ).astype(jnp.bfloat16)
        )
        previous_rows = normed[:, 0]
        previous_all = normed_all[:, 0]
    mixing_output = jnp.concatenate(results, 1)
    return (
        mixing_output,
        present_symbol.reshape(group_partition * CHANNEL_SPAN * CHANNEL_SPAN, narrow_rows),
    )


def solution(mesh):
    placed = (
        P("wide", None, "narrow"),
        P("wide", "narrow"),
        P("narrow"),
        P("narrow"),
        P(None, "narrow"),
        P("narrow", None),
        P(None, None, "narrow"),
        P("narrow", None),
        P(None, "wide"),
        P("wide"),
        P("wide"),
        P("narrow", "wide"),
        P("narrow", "wide"),
        P("narrow", "wide"),
        P("narrow", "wide"),
        P(None, "wide"),
        P("wide"),
        P("wide"),
        P("wide", "narrow"),
    )
    return jax.shard_map(
        per_device,
        mesh=mesh,
        in_specs=placed,
        out_specs=(P("narrow", None, "wide"), P("wide", "narrow")),
        check_vma=False,
    )
```

profile of v0, /device:TPU:8, one launch (start us, length us, event | category | flops | bytes accessed | tf_op | source)
XLA Modules:
  0.0 1447.9 jit_solution(15403730953367358589)
XLA Ops:
  8.7 14.8 %all-reduce.2 = (f32[16,1]{0,1:T(1,128)S(1)}, f32[16,1]{0,1:T(1,128)S(1)}, f32[16,1]{0,1:T(1,128)S(1)}, f32[16,1]{0,1:T(1,128)S(1)}, f32[16,1]{0,1:T(1,128)S(1)}...) all-reduce(f32[16,1]{0,1:T(1,128)S(1)} %bitcast.846, ...), channel_id=1, replica_groups=mesh['wide'=64,'narrow'=8] {'narrow'}, use_global_device_ids=true, to_apply=%region_13.14 | all-reduce | flops 128 | bytes 1024 | tf_op jit(solution)/shard_map/psum | solution.py:49
  33.1 24.0 %all-reduce.1 = (f32[16,1,160]{2,0,1:T(8,128)S(1)}, f32[16,1,160]{2,0,1:T(8,128)S(1)}, f32[16,1,160]{2,0,1:T(8,128)S(1)}, f32[16,1,160]{2,0,1:T(8,128)S(1)}) all-reduce(f32[16,1,160]{2,0,1:T(8,128)S(1)} %convolution_bitcast_fusion.1, ...), channel_id=1, replica_groups=mesh['wide'=64,'narrow'=8] {'narrow'}, use_global_device_ids=true, to_apply=%region_24.25 | all-reduce | flops 10240 | bytes 81920 | tf_op jit(solution)/shard_map/psum | solution.py:68
  61.9 24.4 %all-reduce = (f32[16,1,64]{2,0,1:T(8,128)S(1)}, f32[16,1,64]{2,0,1:T(8,128)S(1)}, f32[16,1,64]{2,0,1:T(8,128)S(1)}, f32[16,1,64]{2,0,1:T(8,128)S(1)}) all-reduce(f32[16,1,64]{2,0,1:T(8,128)S(1)} %convolution_bitcast_fusion.5, f32[16,1,64]{2,0,1:T(8,128)S(1)} %convolution_bitcast_fusion.6, ...), channel_id=1, replica_groups=mesh['wide'=64,'narrow'=8] {'narrow'}, use_global_device_ids=true, to_apply=%region_25.26 | all-reduce | flops 4096 | bytes 32768 | tf_op jit(solution)/shard_map/psum | solution.py:84
  86.4 103.3 %all_gather.50 = bf16[1024,1,192]{2,0,1:T(8,128)(2,1)S(1)} all-gather(bf16[16,1,192]{2,0,1:T(8,128)(2,1)S(1)} %pad_maximum_fusion.4), channel_id=1, replica_groups=mesh['wide'=64,'narrow'=8] {'wide'}, dimensions={0}, use_global_device_ids=true | all-gather | bytes 399360 | tf_op jit(solution)/shard_map/all_gather | solution.py:87
  189.7 99.2 %all_gather.41 = bf16[1024,1,192]{2,0,1:T(8,128)(2,1)S(1)} all-gather(bf16[16,1,192]{2,0,1:T(8,128)(2,1)S(1)} %pad_maximum_fusion.1), channel_id=1, replica_groups=mesh['wide'=64,'narrow'=8] {'wide'}, dimensions={0}, use_global_device_ids=true | all-gather | bytes 399360 | tf_op jit(solution)/shard_map/all_gather | solution.py:87
  288.9 97.0 %all_gather.44 = bf16[1024,1,192]{2,0,1:T(8,128)(2,1)S(1)} all-gather(bf16[16,1,192]{2,0,1:T(8,128)(2,1)S(1)} %pad_maximum_fusion.2), channel_id=1, replica_groups=mesh['wide'=64,'narrow'=8] {'wide'}, dimensions={0}, use_global_device_ids=true | all-gather | bytes 399360 | tf_op jit(solution)/shard_map/all_gather | solution.py:87
  385.9 99.0 %all_gather.47 = bf16[1024,1,192]{2,0,1:T(8,128)(2,1)S(1)} all-gather(bf16[16,1,192]{2,0,1:T(8,128)(2,1)S(1)} %pad_maximum_fusion.3), channel_id=1, replica_groups=mesh['wide'=64,'narrow'=8] {'wide'}, dimensions={0}, use_global_device_ids=true | all-gather | bytes 399360 | tf_op jit(solution)/shard_map/all_gather | solution.py:87
  487.3 2.4 fusion.75
  489.7 2.4 fusion.74
  492.2 2.3 fusion.73
  498.1 81.7 %all-gather.10.cloned.1.call-done = bf16[1024,1,512]{2,0,1:T(8,128)(2,1)} async-done(((bf16[16,1,512]{2,0,1:T(8,128)(2,1)}), bf16[1024,1,512]{2,0,1:T(8,128)(2,1)}) %all-gather.10.cloned.1.call-update) | async-done | bytes 1048592 | tf_op jit(solution)/shard_map/all_gather | solution.py:86
  579.9 2.4 fusion.63
  582.3 2.4 fusion.62
  584.7 2.4 fusion.61
  590.5 127.2 %all-gather.16.cloned.1.call-done = bf16[1024,1,512]{2,0,1:T(8,128)(2,1)} async-done(((bf16[16,1,512]{2,0,1:T(8,128)(2,1)}), bf16[1024,1,512]{2,0,1:T(8,128)(2,1)}) %all-gather.16.cloned.1.call-update) | async-done | bytes 1048592 | tf_op jit(solution)/shard_map/all_gather | solution.py:86
  717.7 2.4 fusion.67
  737.2 14.9 %reduce-scatter.19.cloned.1.call-done = bf16[128,256]{1,0:T(8,128)(2,1)} async-done(((bf16[1024,256]{1,0:T(8,128)(2,1)}), bf16[128,256]{1,0:T(8,128)(2,1)}) %reduce-scatter.19.cloned.1.call-update) | async-done | bytes 65552
  753.0 39.6 %reduce-scatter.13.cloned.1.call-done = bf16[128,256]{1,0:T(8,128)(2,1)} async-done(((bf16[1024,256]{1,0:T(8,128)(2,1)}), bf16[128,256]{1,0:T(8,128)(2,1)}) %reduce-scatter.13.cloned.1.call-update) | async-done | bytes 65552
  793.6 39.4 %reduce-scatter.15.cloned.1.call-done = bf16[128,256]{1,0:T(8,128)(2,1)} async-done(((bf16[1024,256]{1,0:T(8,128)(2,1)}), bf16[128,256]{1,0:T(8,128)(2,1)}) %reduce-scatter.15.cloned.1.call-update) | async-done | bytes 65552
  834.0 40.1 %reduce-scatter.17.cloned.1.call-done = bf16[128,256]{1,0:T(8,128)(2,1)} async-done(((bf16[1024,256]{1,0:T(8,128)(2,1)}), bf16[128,256]{1,0:T(8,128)(2,1)}) %reduce-scatter.17.cloned.1.call-update) | async-done | bytes 65552
  886.4 138.9 %all-gather.14.cloned.1.call-done = bf16[128,1,4096]{0,2,1:T(8,128)(2,1)} async-done(((bf16[128,1,64]{0,2,1:T(8,128)(2,1)}), bf16[128,1,4096]{0,2,1:T(8,128)(2,1)}) %all-gather.14.cloned.1.call-update) | async-done | bytes 1048592 | tf_op jit(solution)/shard_map/all_gather | solution.py:164
  1026.9 136.4 %all-gather.18.cloned.1.call-done = bf16[128,1,4096]{0,2,1:T(8,128)(2,1)} async-done(((bf16[128,1,64]{0,2,1:T(8,128)(2,1)}), bf16[128,1,4096]{0,2,1:T(8,128)(2,1)}) %all-gather.18.cloned.1.call-update) | async-done | bytes 1048592 | tf_op jit(solution)/shard_map/all_gather | solution.py:164
  1164.9 136.3 %all-gather.22.cloned.1.call-done = bf16[128,1,4096]{0,2,1:T(8,128)(2,1)} async-done(((bf16[128,1,64]{0,2,1:T(8,128)(2,1)}), bf16[128,1,4096]{0,2,1:T(8,128)(2,1)}) %all-gather.22.cloned.1.call-update) | async-done | bytes 1048592 | tf_op jit(solution)/shard_map/all_gather | solution.py:164
  1302.7 136.4 %all-gather.26.cloned.1.call-done = bf16[128,1,4096]{0,2,1:T(8,128)(2,1)} async-done(((bf16[128,1,64]{0,2,1:T(8,128)(2,1)}), bf16[128,1,4096]{0,2,1:T(8,128)(2,1)}) %all-gather.26.cloned.1.call-update) | async-done | bytes 1048592 | tf_op jit(solution)/shard_map/all_gather | solution.py:164
  (170 shorter events, 63.7 us)
Async XLA Ops:
  7.2 1018.2 %copy-start = (bf16[4096,64]{0,1:T(8,128)(2,1)S(1)}, bf16[4096,64]{0,1:T(8,128)(2,1)}, u32[]{:S(2)}) copy-start(bf16[4096,64]{0,1:T(8,128)(2,1)} %param.34) | copy-start | bytes 1572868
  7.2 52.3 %copy-start.4 = (bf16[16,512]{1,0:T(8,128)(2,1)S(1)}, bf16[16,512]{1,0:T(8,128)(2,1)}, u32[]{:S(2)}) copy-start(bf16[16,512]{1,0:T(8,128)(2,1)} %param.20) | copy-start | bytes 49156
  7.2 52.3 %copy-start.2 = (bf16[512,64]{0,1:T(8,128)(2,1)S(1)}, bf16[512,64]{0,1:T(8,128)(2,1)}, u32[]{:S(2)}) copy-start(bf16[512,64]{0,1:T(8,128)(2,1)} %param.26) | copy-start | bytes 196612
  7.2 54.5 %copy-start.7 = (f32[64]{0:T(128)S(1)}, f32[64]{0:T(128)}, u32[]{:S(2)}) copy-start(f32[64]{0:T(128)} %param.29) | copy-start | bytes 772
  7.2 480.1 %all-gather.24.cloned.1.call-start = ((), (), s32[]{:S(2)}) async-start(), calls=%async_computation.11 | async-start | bytes 1064960 | tf_op jit(solution)/shard_map/all_gather | solution.py:86
  25.0 462.3 %all-gather.20.cloned.1.call-start = ((), (), s32[]{:S(2)}) async-start(), calls=%async_computation.9 | async-start | bytes 1064960 | tf_op jit(solution)/shard_map/all_gather | solution.py:86
  25.7 472.4 %all-gather.12.cloned.1.call-start = ((), (), s32[]{:S(2)}) async-start(), calls=%async_computation.5 | async-start | bytes 1064960 | tf_op jit(solution)/shard_map/all_gather | solution.py:36
  26.5 553.4 %all-gather.10.cloned.1.call-start = ((), (), s32[]{:S(2)}) async-start(), calls=%async_computation.4 | async-start | bytes 1064960 | tf_op jit(solution)/shard_map/all_gather | solution.py:86
  27.1 690.7 %all-gather.16.cloned.1.call-start = ((), (), s32[]{:S(2)}) async-start(), calls=%async_computation.7 | async-start | bytes 1064960 | tf_op jit(solution)/shard_map/all_gather | solution.py:86
  27.6 724.4 %reduce-scatter.19.cloned.1.call-start = ((), (), s32[]{:S(2)}) async-start(), calls=%async_computation.16 | async-start | bytes 589824
  86.3 399.3 %copy-start.3 = (bf16[64,64]{1,0:T(8,128)(2,1)S(1)}, bf16[64,64]{1,0:T(8,128)(2,1)}, u32[]{:S(2)}) copy-start(bf16[64,64]{1,0:T(8,128)(2,1)} %param.27) | copy-start | bytes 24580
  86.4 399.3 %copy-start.6 = (f32[64]{0:T(128)S(1)}, f32[64]{0:T(128)}, u32[]{:S(2)}) copy-start(f32[64]{0:T(128)} %param.28) | copy-start | bytes 772
  489.7 2.5 copy-start.5
  489.7 2.5 copy-start.15
  497.8 84.4 %copy-start.13 = (bf16[512,64]{0,1:T(8,128)(2,1)S(1)}, bf16[512,64]{0,1:T(8,128)(2,1)}, u32[]{:S(2)}) copy-start(bf16[512,64]{0,1:T(8,128)(2,1)} %param.32) | copy-start | bytes 196612
  497.9 294.8 %reduce-scatter.13.cloned.1.call-start = ((), (), s32[]{:S(2)}) async-start(), calls=%async_computation.13 | async-start | bytes 589824
  589.4 128.4 %copy-start.12 = (bf16[512,64]{0,1:T(8,128)(2,1)S(1)}, bf16[512,64]{0,1:T(8,128)(2,1)}, u32[]{:S(2)}) copy-start(bf16[512,64]{0,1:T(8,128)(2,1)} %param.33) | copy-start | bytes 196612
  590.4 242.6 %reduce-scatter.15.cloned.1.call-start = ((), (), s32[]{:S(2)}) async-start(), calls=%async_computation.14 | async-start | bytes 589824
  717.7 2.5 copy-start.11
  727.3 146.8 %reduce-scatter.17.cloned.1.call-start = ((), (), s32[]{:S(2)}) async-start(), calls=%async_computation.15 | async-start | bytes 589824
  736.9 288.5 %all-gather.14.cloned.1.call-start = ((), (), s32[]{:S(2)}) async-start(), calls=%async_computation.6 | async-start | bytes 1064960 | tf_op jit(solution)/shard_map/all_gather | solution.py:164
  884.4 279.0 %all-gather.18.cloned.1.call-start = ((), (), s32[]{:S(2)}) async-start(), calls=%async_computation.8 | async-start | bytes 1064960 | tf_op jit(solution)/shard_map/all_gather | solution.py:164
  885.1 416.1 %all-gather.22.cloned.1.call-start = ((), (), s32[]{:S(2)}) async-start(), calls=%async_computation.10 | async-start | bytes 1064960 | tf_op jit(solution)/shard_map/all_gather | solution.py:164
  885.7 553.5 %all-gather.26.cloned.1.call-start = ((), (), s32[]{:S(2)}) async-start(), calls=%async_computation.12 | async-start | bytes 1064960 | tf_op jit(solution)/shard_map/all_gather | solution.py:164
  (9 other events, 18.9 us)
Sparse Core Ops, SparseCore 0:
  25.1 140.8 all-gather.23
  168.9 134.9 all-gather.19
  306.8 135.0 all-gather.11
  444.7 135.1 all-gather.9
  582.7 134.9 all-gather.15
  720.4 31.6 reduce-scatter.18
  755.1 37.5 reduce-scatter.12
  795.5 37.4 reduce-scatter.14
  836.6 37.5 reduce-scatter.16
  884.5 140.8 all-gather.13
  1028.3 134.9 all-gather.17
  1166.2 134.9 all-gather.21
  1304.1 134.9 all-gather.25
where the time goes:
time: 1450 us
  waiting for transfers between devices  896 us (62%)
  blocking collectives  462 us (32%)
  matrix products  51.9 us (4%)
  between operations  14.7 us (1%)
    all_gather x4, waiting for transfers between devices, per_device(): lax.all_gather(gated, 'wide', axis=2, tiled=True)  548 us
    all_gather x4, blocking collectives, per_device(): prepare_small_all = lax.all_gather(small, 'wide', axis=0, tiled=True)  398 us
    all_gather x4, waiting for transfers between devices, per_device(): prepare_normed_all = lax.all_gather(normed, 'wide', axis=0, tiled=True)  209 us
    unnamed x17, waiting for transfers between devices  138 us
    dot_general x16, matrix products, per_device(): jnp.einsum('smd,de->sme', mixed_input, weights[selector_index], preferred...  35.5 us
  transfers between devices with their start and end apart: 13, of which 10 were waited for; matrix products, arithmetic and copies ran while one was open for 4% of the time, Pallas kernels for 0%

commit v1 on v0

--- a/solution.py
+++ b/solution.py
@@ -1,3 +1,4 @@
+import functools
 import jax
 import jax.numpy as jnp
 from jax import lax
@@ -5,6 +6,20 @@
 
 CHANNEL_SPAN = 64
 FEATURE_EXTENT = 4096
+
+
+def marks_play(sheet, axis_id):
+    k_all = jax.lax.axis_size(axis_id)
+    return jax.lax.all_to_all(
+        jnp.tile(sheet, list(map(lambda tick: k_all if tick == 2 else 1, range(sheet.ndim)))),
+        axis_id,
+        split_axis=2,
+        concat_axis=2,
+        tiled=True,
+    )
+
+
+tell_wall = functools.partial(marks_play, axis_id="wide")
 
 
 def per_device(
@@ -161,7 +176,7 @@
         results.append(
             jnp.einsum(
                 "smc,ce->sme",
-                lax.all_gather(gated, "wide", axis=2, tiled=True),
+                tell_wall(gated),
                 emission_projection,
                 preferred_element_type=jnp.float32,
             ).astype(jnp.bfloat16)

time: 1450 us -> 1210 us (0.83)
  the two profiles are of different devices: /device:TPU:8 before, /device:TPU:24 now
where the time goes in v1:
time: 1210 us; the launch traced here: 1200 us
  blocking collectives  461 us (38%)
  waiting for transfers between devices  403 us (33%)
  local copies, waits for them, and re-layouts  131 us (11%)
  other arithmetic  104 us (9%)
  matrix products  52.7 us (4%)
  starting transfers between devices  35.3 us (3%)
  between operations  15 us (1%)
    all_gather x4, blocking collectives, per_device(): prepare_small_all = lax.all_gather(small, 'wide', axis=0, tiled=True)  398 us
    unnamed x13, waiting for transfers between devices  146 us
    all_gather x4, waiting for transfers between devices, per_device(): prepare_normed_all = lax.all_gather(normed, 'wide', axis=0, tiled=True)  128 us
    unnamed x8, other arithmetic  93.7 us
    all_gather x1, waiting for transfers between devices, per_device(): lax.all_gather(prior_symbol_memory, 'wide', axis=0, tiled=True)  71.7 us
    another operation x8, local copies, waits for them, and re-layouts, marks_play(): jnp.tile(sheet, list(map(lambda tick: k_all if tick == 2 else 1, range(sh...  67.9 us
    all_to_all x4, waiting for transfers between devices, marks_play(): jax.lax.all_to_all(jnp.tile(sheet, list(map(lambda tick: k_all if tick ==...  56.7 us
    unnamed x67, local copies, waits for them, and re-layouts  44.1 us
  transfers between devices with their start and end apart: 13, of which 10 were waited for; matrix products, arithmetic and copies ran while one was open for 18% of the time, Pallas kernels for 0%

profile of v1, /device:TPU:24, one launch (start us, length us, event | category | flops | bytes accessed | tf_op | source)
XLA Modules:
  0.0 1200.9 jit_solution(9012834429346026926)
XLA Ops:
  8.7 14.1 %all-reduce.2 = (f32[16,1]{0,1:T(1,128)S(1)}, f32[16,1]{0,1:T(1,128)S(1)}, f32[16,1]{0,1:T(1,128)S(1)}, f32[16,1]{0,1:T(1,128)S(1)}, f32[16,1]{0,1:T(1,128)S(1)}...) all-reduce(f32[16,1]{0,1:T(1,128)S(1)} %bitcast.898, ...), channel_id=1, replica_groups=mesh['wide'=64,'narrow'=8] {'narrow'}, use_global_device_ids=true, to_apply=%region_13.14 | all-reduce | flops 128 | bytes 1024 | tf_op jit(solution)/shard_map/psum | solution.py:64
  32.4 24.9 %all-reduce.1 = (f32[16,1,160]{2,0,1:T(8,128)S(1)}, f32[16,1,160]{2,0,1:T(8,128)S(1)}, f32[16,1,160]{2,0,1:T(8,128)S(1)}, f32[16,1,160]{2,0,1:T(8,128)S(1)}) all-reduce(f32[16,1,160]{2,0,1:T(8,128)S(1)} %convolution_bitcast_fusion.1, ...), channel_id=1, replica_groups=mesh['wide'=64,'narrow'=8] {'narrow'}, use_global_device_ids=true, to_apply=%region_24.25 | all-reduce | flops 10240 | bytes 81920 | tf_op jit(solution)/shard_map/psum | solution.py:83
  61.9 23.3 %all-reduce = (f32[16,1,64]{2,0,1:T(8,128)S(1)}, f32[16,1,64]{2,0,1:T(8,128)S(1)}, f32[16,1,64]{2,0,1:T(8,128)S(1)}, f32[16,1,64]{2,0,1:T(8,128)S(1)}) all-reduce(f32[16,1,64]{2,0,1:T(8,128)S(1)} %convolution_bitcast_fusion.5, f32[16,1,64]{2,0,1:T(8,128)S(1)} %convolution_bitcast_fusion.6, ...), channel_id=1, replica_groups=mesh['wide'=64,'narrow'=8] {'narrow'}, use_global_device_ids=true, to_apply=%region_25.26 | all-reduce | flops 4096 | bytes 32768 | tf_op jit(solution)/shard_map/psum | solution.py:99
  85.2 103.1 %all_gather.33 = bf16[1024,1,192]{2,0,1:T(8,128)(2,1)S(1)} all-gather(bf16[16,1,192]{2,0,1:T(8,128)(2,1)S(1)} %pad_maximum_fusion.3), channel_id=1, replica_groups=mesh['wide'=64,'narrow'=8] {'wide'}, dimensions={0}, use_global_device_ids=true | all-gather | bytes 399360 | tf_op jit(solution)/shard_map/all_gather | solution.py:102
  188.4 99.3 %all_gather.31 = bf16[1024,1,192]{2,0,1:T(8,128)(2,1)S(1)} all-gather(bf16[16,1,192]{2,0,1:T(8,128)(2,1)S(1)} %pad_maximum_fusion.2), channel_id=1, replica_groups=mesh['wide'=64,'narrow'=8] {'wide'}, dimensions={0}, use_global_device_ids=true | all-gather | bytes 399360 | tf_op jit(solution)/shard_map/all_gather | solution.py:102
  287.7 96.8 %all_gather.29 = bf16[1024,1,192]{2,0,1:T(8,128)(2,1)S(1)} all-gather(bf16[16,1,192]{2,0,1:T(8,128)(2,1)S(1)} %pad_maximum_fusion.1), channel_id=1, replica_groups=mesh['wide'=64,'narrow'=8] {'wide'}, dimensions={0}, use_global_device_ids=true | all-gather | bytes 399360 | tf_op jit(solution)/shard_map/all_gather | solution.py:102
  384.6 99.3 %all_gather.35 = bf16[1024,1,192]{2,0,1:T(8,128)(2,1)S(1)} all-gather(bf16[16,1,192]{2,0,1:T(8,128)(2,1)S(1)} %pad_maximum_fusion.4), channel_id=1, replica_groups=mesh['wide'=64,'narrow'=8] {'wide'}, dimensions={0}, use_global_device_ids=true | all-gather | bytes 399360 | tf_op jit(solution)/shard_map/all_gather | solution.py:102
  508.0 71.7 %all-gather.8.cloned.1.call-done = bf16[1024,512]{1,0:T(8,128)(2,1)} async-done(((bf16[16,512]{1,0:T(8,128)(2,1)}), bf16[1024,512]{1,0:T(8,128)(2,1)}) %all-gather.8.cloned.1.call-update) | async-done | bytes 1048592 | tf_op jit(solution)/shard_map/all_gather | solution.py:51
  590.3 127.8 %all-gather.14.cloned.1.call-done = bf16[1024,1,512]{2,0,1:T(8,128)(2,1)} async-done(((bf16[16,1,512]{2,0,1:T(8,128)(2,1)}), bf16[1024,1,512]{2,0,1:T(8,128)(2,1)}) %all-gather.14.cloned.1.call-update) | async-done | bytes 1048592 | tf_op jit(solution)/shard_map/all_gather | solution.py:101
  727.7 25.3 %reduce-scatter.17.cloned.1.call-done = bf16[128,256]{1,0:T(8,128)(2,1)} async-done(((bf16[1024,256]{1,0:T(8,128)(2,1)}), bf16[128,256]{1,0:T(8,128)(2,1)}) %reduce-scatter.17.cloned.1.call-update) | async-done | bytes 65552
  754.0 39.6 %reduce-scatter.15.cloned.1.call-done = bf16[128,256]{1,0:T(8,128)(2,1)} async-done(((bf16[1024,256]{1,0:T(8,128)(2,1)}), bf16[128,256]{1,0:T(8,128)(2,1)}) %reduce-scatter.15.cloned.1.call-update) | async-done | bytes 65552
  794.6 39.4 %reduce-scatter.13.cloned.1.call-done = bf16[128,256]{1,0:T(8,128)(2,1)} async-done(((bf16[1024,256]{1,0:T(8,128)(2,1)}), bf16[128,256]{1,0:T(8,128)(2,1)}) %reduce-scatter.13.cloned.1.call-update) | async-done | bytes 65552
  835.0 39.6 %reduce-scatter.19.cloned.1.call-done = bf16[128,256]{1,0:T(8,128)(2,1)} async-done(((bf16[1024,256]{1,0:T(8,128)(2,1)}), bf16[128,256]{1,0:T(8,128)(2,1)}) %reduce-scatter.19.cloned.1.call-update) | async-done | bytes 65552
  884.6 16.7 %copy.89 = bf16[128,1,4096]{0,1,2:T(2,128)(2,1)S(1)} copy(bf16[128,1,4096]{0,2,1:T(8,128)(2,1)S(1)} %bitcast.885) | data formatting | bytes 2097152 | tf_op jit(solution)/shard_map/tile | solution.py:14
  901.8 23.4 %reduce.28 = bf16[4096,128]{1,0:T(8,128)(2,1)} reduce(bf16[4096,1,128]{2,1,0:T(2,128)(2,1)S(1)} %bitcast.881, bf16[]{:T(256)} %broadcast.911), dimensions={1}, to_apply=%bitcast.872.reduce_sub_computation | reduce | bytes 2097154
  927.4 16.3 %all-to-all-start.3 = ((bf16[64,2,4096]{2,1,0:T(2,128)(2,1)}), bf16[64,2,4096]{2,1,0:T(2,128)(2,1)}, u32[]{:S(2)}, u32[]{:S(2)}) async-start(bf16[64,2,4096]{2,1,0:T(2,128)(2,1)} %reshape.1586), calls=%async_computation.3 | async-start | bytes 2097152 | tf_op jit(solution)/shard_map/all_to_all | solution.py:13
  943.9 16.7 %copy.90 = bf16[128,1,4096]{0,1,2:T(2,128)(2,1)S(1)} copy(bf16[128,1,4096]{0,2,1:T(8,128)(2,1)S(1)} %bitcast.886) | data formatting | bytes 2097152 | tf_op jit(solution)/shard_map/tile | solution.py:14
  960.7 23.4 %reduce.29 = bf16[4096,128]{1,0:T(8,128)(2,1)} reduce(bf16[4096,1,128]{2,1,0:T(2,128)(2,1)S(1)} %bitcast.883, bf16[]{:T(256)} %broadcast.911), dimensions={1}, to_apply=%bitcast.873.reduce_sub_computation | reduce | bytes 2097154
  986.2 13.9 %all-to-all-done.3 = bf16[64,2,4096]{2,1,0:T(2,128)(2,1)} async-done(((bf16[64,2,4096]{2,1,0:T(2,128)(2,1)}), bf16[64,2,4096]{2,1,0:T(2,128)(2,1)}, u32[]{:S(2)}, u32[]{:S(2)}) %all-to-all-start.3) | async-done | bytes 1048608 | tf_op jit(solution)/shard_map/all_to_all | solution.py:13
  1006.4 16.7 %copy.91 = bf16[128,1,4096]{0,1,2:T(2,128)(2,1)S(1)} copy(bf16[128,1,4096]{0,2,1:T(8,128)(2,1)S(1)} %bitcast.887) | data formatting | bytes 2097152 | tf_op jit(solution)/shard_map/tile | solution.py:14
  1023.2 23.4 %reduce.30 = bf16[4096,128]{1,0:T(8,128)(2,1)} reduce(bf16[4096,1,128]{2,1,0:T(2,128)(2,1)S(1)} %bitcast.884, bf16[]{:T(256)} %broadcast.911), dimensions={1}, to_apply=%bitcast.874.reduce_sub_computation | reduce | bytes 2097154
  1067.5 16.7 %copy.92 = bf16[128,1,4096]{0,1,2:T(2,128)(2,1)S(1)} copy(bf16[128,1,4096]{0,2,1:T(8,128)(2,1)S(1)} %bitcast.888) | data formatting | bytes 2097152 | tf_op jit(solution)/shard_map/tile | solution.py:14
  1084.3 23.4 %reduce.31 = bf16[4096,128]{1,0:T(8,128)(2,1)} reduce(bf16[4096,1,128]{2,1,0:T(2,128)(2,1)S(1)} %bitcast.882, bf16[]{:T(256)} %broadcast.911), dimensions={1}, to_apply=%bitcast.875.reduce_sub_computation | reduce | bytes 2097154
  1162.8 18.6 %all-to-all-done = bf16[64,2,4096]{2,1,0:T(2,128)(2,1)} async-done(((bf16[64,2,4096]{2,1,0:T(2,128)(2,1)}), bf16[64,2,4096]{2,1,0:T(2,128)(2,1)}, u32[]{:S(2)}, u32[]{:S(2)}) %all-to-all-start) | async-done | bytes 1048608 | tf_op jit(solution)/shard_map/all_to_all | solution.py:13
  (201 shorter events, 172.5 us)
Async XLA Ops:
  7.2 1151.7 %copy-start = (bf16[4096,64]{0,1:T(8,128)(2,1)S(1)}, bf16[4096,64]{0,1:T(8,128)(2,1)}, u32[]{:S(2)}) copy-start(bf16[4096,64]{0,1:T(8,128)(2,1)} %param.34) | copy-start | bytes 1572868
  7.2 52.5 %copy-start.5 = (bf16[16,512]{1,0:T(8,128)(2,1)S(1)}, bf16[16,512]{1,0:T(8,128)(2,1)}, u32[]{:S(2)}) copy-start(bf16[16,512]{1,0:T(8,128)(2,1)} %param.20) | copy-start | bytes 49156
  7.2 52.5 %copy-start.3 = (bf16[512,64]{0,1:T(8,128)(2,1)S(1)}, bf16[512,64]{0,1:T(8,128)(2,1)}, u32[]{:S(2)}) copy-start(bf16[512,64]{0,1:T(8,128)(2,1)} %param.26) | copy-start | bytes 196612
  7.2 479.2 %all-gather.10.cloned.1.call-start = ((), (), s32[]{:S(2)}) async-start(), calls=%async_computation.10 | async-start | bytes 1064960 | tf_op jit(solution)/shard_map/all_gather | solution.py:101
  24.3 462.1 %all-gather.12.cloned.1.call-start = ((), (), s32[]{:S(2)}) async-start(), calls=%async_computation.11 | async-start | bytes 1064960 | tf_op jit(solution)/shard_map/all_gather | solution.py:101
  25.0 472.3 %all-gather.6.cloned.1.call-start = ((), (), s32[]{:S(2)}) async-start(), calls=%async_computation.8 | async-start | bytes 1064960 | tf_op jit(solution)/shard_map/all_gather | solution.py:101
  25.8 553.9 %all-gather.8.cloned.1.call-start = ((), (), s32[]{:S(2)}) async-start(), calls=%async_computation.9 | async-start | bytes 1064960 | tf_op jit(solution)/shard_map/all_gather | solution.py:51
  26.3 691.8 %all-gather.14.cloned.1.call-start = ((), (), s32[]{:S(2)}) async-start(), calls=%async_computation.12 | async-start | bytes 1064960 | tf_op jit(solution)/shard_map/all_gather | solution.py:101
  26.9 726.1 %reduce-scatter.17.cloned.1.call-start = ((), (), s32[]{:S(2)}) async-start(), calls=%async_computation.15 | async-start | bytes 589824
  59.7 424.1 %copy-start.10 = (f32[64]{0:T(128)S(1)}, f32[64]{0:T(128)}, u32[]{:S(2)}) copy-start(f32[64]{0:T(128)} %param.29) | copy-start | bytes 772
  85.2 399.5 %copy-start.4 = (bf16[64,64]{1,0:T(8,128)(2,1)S(1)}, bf16[64,64]{1,0:T(8,128)(2,1)}, u32[]{:S(2)}) copy-start(bf16[64,64]{1,0:T(8,128)(2,1)} %param.27) | copy-start | bytes 24580
  85.2 399.5 %copy-start.9 = (f32[64]{0:T(128)S(1)}, f32[64]{0:T(128)}, u32[]{:S(2)}) copy-start(f32[64]{0:T(128)} %param.28) | copy-start | bytes 772
  497.1 2.7 copy-start.15
  497.1 296.5 %reduce-scatter.15.cloned.1.call-start = ((), (), s32[]{:S(2)}) async-start(), calls=%async_computation.14 | async-start | bytes 589824
  506.8 72.8 %copy-start.7 = (bf16[5,32,512]{2,1,0:T(8,128)(2,1)S(1)}, bf16[5,32,512]{2,1,0:T(8,128)(2,1)}, u32[]{:S(2)}) copy-start(bf16[5,32,512]{2,1,0:T(8,128)(2,1)} %param.25) | copy-start | bytes 491524
  507.9 74.2 %copy-start.16 = (bf16[512,64]{0,1:T(8,128)(2,1)S(1)}, bf16[512,64]{0,1:T(8,128)(2,1)}, u32[]{:S(2)}) copy-start(bf16[512,64]{0,1:T(8,128)(2,1)} %param.32) | copy-start | bytes 196612
  507.9 326.0 %reduce-scatter.13.cloned.1.call-start = ((), (), s32[]{:S(2)}) async-start(), calls=%async_computation.13 | async-start | bytes 589824
  590.2 130.2 %copy-start.13 = (bf16[1024,1,512]{2,0,1:T(8,128)(2,1)S(1)}, bf16[1024,1,512]{2,0,1:T(8,128)(2,1)}, u32[]{:S(2)}) copy-start(bf16[1024,1,512]{2,0,1:T(8,128)(2,1)} %all-gather.12.cloned.1.call-done) | copy-start | bytes 3145732
  590.3 284.3 %reduce-scatter.19.cloned.1.call-start = ((), (), s32[]{:S(2)}) async-start(), calls=%async_computation.16 | async-start | bytes 589824
  927.4 72.7 %all-to-all-start.3 = ((bf16[64,2,4096]{2,1,0:T(2,128)(2,1)}), bf16[64,2,4096]{2,1,0:T(2,128)(2,1)}, u32[]{:S(2)}, u32[]{:S(2)}) async-start(bf16[64,2,4096]{2,1,0:T(2,128)(2,1)} %reshape.1586), calls=%async_computation.3 | async-start | bytes 2097152 | tf_op jit(solution)/shard_map/all_to_all | solution.py:13
  1000.1 60.9 %all-to-all-start.2 = ((bf16[64,2,4096]{2,1,0:T(2,128)(2,1)}), bf16[64,2,4096]{2,1,0:T(2,128)(2,1)}, u32[]{:S(2)}, u32[]{:S(2)}) async-start(bf16[64,2,4096]{2,1,0:T(2,128)(2,1)} %reshape.1588), calls=%async_computation.2 | async-start | bytes 2097152 | tf_op jit(solution)/shard_map/all_to_all | solution.py:13
  1061.0 60.7 %all-to-all-start.1 = ((bf16[64,2,4096]{2,1,0:T(2,128)(2,1)}), bf16[64,2,4096]{2,1,0:T(2,128)(2,1)}, u32[]{:S(2)}, u32[]{:S(2)}) async-start(bf16[64,2,4096]{2,1,0:T(2,128)(2,1)} %reshape.1590), calls=%async_computation.1 | async-start | bytes 2097152 | tf_op jit(solution)/shard_map/all_to_all | solution.py:13
  1121.8 59.7 %all-to-all-start = ((bf16[64,2,4096]{2,1,0:T(2,128)(2,1)}), bf16[64,2,4096]{2,1,0:T(2,128)(2,1)}, u32[]{:S(2)}, u32[]{:S(2)}) async-start(bf16[64,2,4096]{2,1,0:T(2,128)(2,1)} %reshape.1592), calls=%async_computation | async-start | bytes 2097152 | tf_op jit(solution)/shard_map/all_to_all | solution.py:13
  1158.8 3.5 copy-start.2
  (14 other events, 31.3 us)
Sparse Core Ops, SparseCore 0:
  24.4 141.3 all-gather.9
  168.7 134.9 all-gather.11
  306.7 134.9 all-gather.5
  444.5 135.0 all-gather.7
  583.0 135.0 all-gather.13
  721.3 31.6 reduce-scatter.16
  756.0 37.5 reduce-scatter.14
  796.4 37.5 reduce-scatter.12
  837.0 37.5 reduce-scatter.18
